TPU v7x, 512 devices: a whole 4x8x8 slice. The times are simulated.
512 devices in a mesh: gx: 16 (over y_hi, x, core), gy: 4 (over y_lo), gz: 8 (over z).
Axes of the slice: x: 4, y: 8 (y_hi: 2, y_lo: 4; y = y_hi * 4 + y_lo), z: 8, core: 2. Of those that a mesh axis runs over, the one named last changes fastest.
Arguments:
- velocity: float32 [3, 32, 4, 32, 512], P(None, 'gx', 'gy', 'gz'), may hold values from -4 to 4
- reaction: float32 [32, 4, 32, 512], P('gx', 'gy', 'gz'), may hold values from 10 to 100
Outputs:
- velocity_out: float32 [3, 32, 4, 32, 512], P(None, 'gx', 'gy', 'gz')
- pressure: float32 [32, 4, 32, 512], P('gx', 'gy', 'gz')
- residual: float32 [32, 4, 32, 512], P('gx', 'gy', 'gz')
All inputs are finite; a program needn't handle non-finite values.
Results may differ from a plain program's by a relative error of at most 0.007.
Values sent between devices are 32-bit elements; how exact they have to be, the bound alone decides.
A program may use at most 64 MiB of HBM per device.

v0:
```python
import jax
import jax.numpy as jnp
import numpy as np
from jax import lax
from jax.sharding import PartitionSpec as P

SUBSTEPS = 2
ITERS = 4
step_size = 0.02


def extended(block, sides, width, periodic):
    for axis, dim in sides:
        count = lax.axis_size(axis)
        forward = [(i, i + 1) for i in range(count - 1)]
        if periodic:
            forward.append((count - 1, 0))
        backward = [(target, source) for source, target in forward]
        low = lax.ppermute(
            lax.slice_in_dim(block, block.shape[dim] - width, None, axis=dim), axis, forward
        )
        high = lax.ppermute(lax.slice_in_dim(block, 0, width, axis=dim), axis, backward)
        block = jnp.concatenate([low, block, high], axis=dim)
    return block


def legendre_seven(points):
    earlier = points * 0.0 + 1.0
    current = points
    for degree in range(1, 7):
        earlier, current = (
            current,
            ((2 * degree + 1) * points * current - degree * earlier) / (degree + 1),
        )
    return current


def tables():
    half = np.array([0.20929921790247888, 0.5917001814331423, 0.8717401485096066, 1.0])
    points = np.concatenate([-half[::-1], half])
    legendre = legendre_seven(points)
    weights = 2.0 / (56.0 * legendre**2)
    spacing = points[:, None] - points[None, :] + np.eye(8)
    derivative = legendre[:, None] / legendre[None, :] / spacing * (1.0 - np.eye(8))
    derivative[0, 0] = -14.0
    derivative[7, 7] = 14.0
    return (jnp.asarray(weights, jnp.float32), jnp.asarray(derivative, jnp.float32))


def derive(values, derivative, along_dim, transposed):
    layout = values.shape
    matrix = derivative.T if transposed else derivative
    blocks = values.reshape(-1, 8, 8, 8)
    patterns = ("aq,nqbc->nabc", "bq,naqc->nabc", "cq,nabq->nabc")
    result = jnp.einsum(patterns[along_dim], matrix, blocks, precision=lax.Precision.HIGHEST)
    return result.reshape(layout)


def place_face(values, target_axis, position, update):
    selector = tuple(
        (position if place == target_axis else slice(None) for place in range(values.ndim))
    )
    return values.at[selector].set(update)


def faces_along_x(sequence):
    return extended(sequence, (("gx", 0),), 1, True)


def faces_along_y(sequence):
    return extended(sequence, (("gy", 0),), 1, False)


def faces_along_z(sequence):
    return extended(sequence, (("gz", 0),), 1, False)


def join_faces(values, along_dim, exchanger):
    lower_face = jnp.moveaxis(jnp.take(values, 0, axis=4 + along_dim), 1 + along_dim, 0)
    upper_face = jnp.moveaxis(jnp.take(values, 7, axis=4 + along_dim), 1 + along_dim, 0)
    elements = lower_face.shape[0]
    face_shape = lower_face.shape
    sequence = jnp.stack([lower_face, upper_face], axis=1).reshape(2 * elements, -1)
    padded = exchanger(sequence)
    paired = padded.reshape(elements + 1, 2, -1)
    totals = paired[:, 0] + paired[:, 1]
    new_lower = jnp.moveaxis(totals[:-1].reshape(face_shape), 0, 1 + along_dim)
    new_upper = jnp.moveaxis(totals[1:].reshape(face_shape), 0, 1 + along_dim)
    values = place_face(values, 4 + along_dim, 0, new_lower)
    return place_face(values, 4 + along_dim, 7, new_upper)


def assemble(values):
    exchangers = (faces_along_x, faces_along_y, faces_along_z)
    dim_order = (0, 1, 2)
    for along_dim in dim_order:
        values = join_faces(values, along_dim, exchangers[along_dim])
    return values


def dim_factors(local_count, offset, total_count, bounded_by_walls):
    element_ids = offset + jnp.arange(local_count)
    node_ids = jnp.arange(8)
    at_end = (node_ids[None, :] == 0) | (node_ids[None, :] == 7)
    low_wall = (element_ids[:, None] == 0) & (node_ids[None, :] == 0)
    high_wall = (element_ids[:, None] == total_count - 1) & (node_ids[None, :] == 7)
    on_wall = (low_wall | high_wall) & bounded_by_walls
    shared = at_end & jnp.logical_not(on_wall)
    return (jnp.where(shared, 2.0, 1.0).astype(jnp.float32), on_wall.astype(jnp.float32))


def body(velocity, reaction):
    weights, derivative = tables()
    count_x, count_y, count_z = (reaction.shape[0], reaction.shape[1], reaction.shape[2])
    speed = velocity.reshape(3, count_x, count_y, count_z, 8, 8, 8)
    react = reaction.reshape(1, count_x, count_y, count_z, 8, 8, 8)
    mass_matrix = weights[:, None, None] * weights[None, :, None] * weights[None, None, :]
    factor_x, wall_x = dim_factors(
        count_x, lax.axis_index("gx") * count_x, lax.axis_size("gx") * count_x, False
    )
    factor_y, wall_y = dim_factors(
        count_y, lax.axis_index("gy") * count_y, lax.axis_size("gy") * count_y, True
    )
    factor_z, wall_z = dim_factors(
        count_z, lax.axis_index("gz") * count_z, lax.axis_size("gz") * count_z, True
    )
    multiplicity = (
        factor_x[None, :, None, None, :, None, None]
        * factor_y[None, None, :, None, None, :, None]
        * factor_z[None, None, None, :, None, None, :]
    )
    interior = (1.0 - wall_y[None, None, :, None, None, :, None]) * (
        1.0 - wall_z[None, None, None, :, None, None, :]
    )
    stiff_sum = jnp.sum(weights[:, None] * derivative * derivative, axis=0)
    diag_local = (
        stiff_sum[:, None, None] * weights[None, :, None] * weights[None, None, :]
        + weights[:, None, None] * stiff_sum[None, :, None] * weights[None, None, :]
        + weights[:, None, None] * weights[None, :, None] * stiff_sum[None, None, :]
    )
    diag_terms = diag_local + react * mass_matrix
    speed = assemble(speed) / multiplicity
    diagonal = None
    for substep in range(SUBSTEPS):
        gradient_fields = [derive(speed, derivative, along_dim, False) for along_dim in range(3)]
        transport = (
            speed[0:1] * gradient_fields[0]
            + speed[1:2] * gradient_fields[1]
            + speed[2:3] * gradient_fields[2]
        )
        tendency = assemble(mass_matrix * transport) / (mass_matrix * multiplicity)
        speed = interior * (speed - step_size * tendency)
    spread = (
        derive(speed[0:1], derivative, 0, False)
        + derive(speed[1:2], derivative, 1, False)
        + derive(speed[2:3], derivative, 2, False)
    )
    source = -assemble(mass_matrix * spread)
    diagonal = assemble(diag_terms)

    def local_inner(first, second):
        return jnp.sum(first * second / multiplicity)

    def norm_weighted_mass(residual_vec, precond_vec):
        return lax.psum(local_inner(residual_vec, precond_vec), ("gx", "gy", "gz"))

    pressure = jnp.zeros_like(source)
    residual = source
    precond = residual / diagonal
    search = precond
    progress = norm_weighted_mass(residual, precond)
    for sweep_index in range(ITERS):
        local_sum = react * mass_matrix * search
        for apply_along_dim in range(3):
            local_sum = local_sum + derive(
                mass_matrix * derive(search, derivative, apply_along_dim, False),
                derivative,
                apply_along_dim,
                True,
            )
        applied = assemble(local_sum)
        step_length = progress / lax.psum(local_inner(search, applied), ("gx", "gy", "gz"))
        pressure = pressure + step_length * search
        residual = residual - step_length * applied
        precond = residual / diagonal
        progress_next = norm_weighted_mass(residual, precond)
        search = precond + progress_next / progress * search
        progress = progress_next
    return (
        speed.reshape(3, count_x, count_y, count_z, 512),
        pressure.reshape(count_x, count_y, count_z, 512),
        residual.reshape(count_x, count_y, count_z, 512),
    )


def solution(mesh):
    in_specs = (P(None, "gx", "gy", "gz", None), P("gx", "gy", "gz", None))
    out_specs = (
        P(None, "gx", "gy", "gz", None),
        P("gx", "gy", "gz", None),
        P("gx", "gy", "gz", None),
    )
    return jax.shard_map(body, mesh=mesh, in_specs=in_specs, out_specs=out_specs, check_vma=False)
```

profile of v0, /device:TPU:1, one launch (start us, length us, event | category | flops | bytes accessed | tf_op | source)
XLA Modules:
  0.0 1127.1 jit_solution(3727668878768256225)
XLA Ops:
  2.1 4.5 collective-permute-start
  6.6 6.2 collective-permute-start.1
  15.8 9.7 collective-permute-start.25
  30.0 4.0 collective-permute-start.2
  35.4 3.0 collective-permute-done.3
  46.6 3.0 collective-permute-done.5
  51.0 2.6 scatter.186
  54.8 15.4 %scatter.189 = f32[3,2,1,4,8,8,8]{6,5,4,3,1,0,2:T(8,128)S(1)} dynamic-update-slice(f32[3,2,1,4,8,8,8]{6,5,4,3,1,0,2:T(8,128)S(1)} %scatter.186, f32[3,2,1,4,8,8,1]{6,5,4,3,1,0,2:T(8,128)S(1)} %copy.186, s32[]{:T(128)} %constant.1319.clone.1, s32[]{:T(128)} %constant.1319.clone.1, s32[]{:T(128)} %constant.1319.clone.1, s32[]{:T(128)} %constant.1319.clone.1, s32[]{:T(128)} %constant.1319.clone.1, ...) | dynamic-update-slice | bytes 12292 | tf_op jit(solution)/shard_map/scatter | solution.py:63
  76.7 2.4 fusion.2
  79.4 2.2 collective-permute-start.6
  81.6 12.9 %collective-permute-start.7 = (f32[1,768]{1,0:T(1,128)S(1)}, f32[1,768]{1,0:T(1,128)S(1)}, u32[]{:S(2)}, u32[]{:S(2)}) collective-permute-start(f32[1,768]{1,0:T(1,128)S(1)} %get-tuple-element.938), channel_id=1, source_target_pairs={{32,0},{64,32},{96,64},{128,96},{160,128},{192,160},{224,192},{256... | collective-permute-start | bytes 9224 | tf_op jit(solution)/shard_map/ppermute | solution.py:22
  95.9 3.2 collective-permute-start.8
  100.8 2.8 collective-permute-done.9
  109.1 4.0 collective-permute-start.10
  114.5 4.7 collective-permute-done.11
  120.1 2.1 copy.201
  122.1 2.6 scatter.196
  127.5 15.4 %scatter.199 = f32[3,2,1,4,8,8,8]{6,5,4,3,1,0,2:T(8,128)S(1)} dynamic-update-slice(f32[3,2,1,4,8,8,8]{6,5,4,3,1,0,2:T(8,128)S(1)} %scatter.196, f32[3,2,1,4,8,8,1]{6,5,4,3,1,0,2:T(8,128)S(1)} %copy.203, s32[]{:T(128)} %constant.1319.clone.1, s32[]{:T(128)} %constant.1319.clone.1, s32[]{:T(128)} %constant.1319.clone.1, s32[]{:T(128)} %constant.1319.clone.1, s32[]{:T(128)} %constant.1319.clone.1, ...) | dynamic-update-slice | bytes 12292 | tf_op jit(solution)/shard_map/scatter | solution.py:63
  148.1 2.2 fusion.5
  152.4 12.7 %collective-permute-start.13 = (f32[1,768]{1,0:T(1,128)S(1)}, f32[1,768]{1,0:T(1,128)S(1)}, u32[]{:S(2)}, u32[]{:S(2)}) collective-permute-start(f32[1,768]{1,0:T(1,128)S(1)} %get-tuple-element.930), channel_id=1, source_target_pairs={{32,0},{64,32},{96,64},{128,96},{160,128},{192,160},{224,192},{256... | collective-permute-start | bytes 9224 | tf_op jit(solution)/shard_map/ppermute | solution.py:22
  165.2 4.8 collective-permute-start.28
  171.9 3.2 collective-permute-start.14
  177.0 2.6 collective-permute-done.15
  185.1 4.3 collective-permute-start.16
  190.7 3.0 collective-permute-done.17
  195.1 2.6 scatter.206
  199.0 15.4 %scatter.209 = f32[3,2,1,4,8,8,8]{6,5,4,3,1,0,2:T(8,128)S(1)} dynamic-update-slice(f32[3,2,1,4,8,8,8]{6,5,4,3,1,0,2:T(8,128)S(1)} %scatter.206, f32[3,2,1,4,8,8,1]{6,5,4,3,1,0,2:T(8,128)S(1)} %copy.220, s32[]{:T(128)} %constant.1319.clone.1, s32[]{:T(128)} %constant.1319.clone.1, s32[]{:T(128)} %constant.1319.clone.1, s32[]{:T(128)} %constant.1319.clone.1, s32[]{:T(128)} %constant.1319.clone.1, ...) | dynamic-update-slice | bytes 12292 | tf_op jit(solution)/shard_map/scatter | solution.py:63
  219.2 12.8 %collective-permute-start.19 = (f32[1,256]{1,0:T(1,128)S(1)}, f32[1,256]{1,0:T(1,128)S(1)}, u32[]{:S(2)}, u32[]{:S(2)}) collective-permute-start(f32[1,256]{1,0:T(1,128)S(1)} %get-tuple-element.992), channel_id=1, source_target_pairs={{32,0},{64,32},{96,64},{128,96},{160,128},{192,160},{224,192},{256... | collective-permute-start | bytes 3080 | tf_op jit(solution)/shard_map/ppermute | solution.py:22
  236.2 3.0 collective-permute-done.21
  240.3 3.6 collective-permute-start.22
  246.7 4.6 scatter.229
  252.8 4.8 scatter.219
  263.0 11.8 %collective-permute-start.31 = (f32[1,256]{1,0:T(1,128)S(1)}, f32[1,256]{1,0:T(1,128)S(1)}, u32[]{:S(2)}, u32[]{:S(2)}) collective-permute-start(f32[1,256]{1,0:T(1,128)S(1)} %get-tuple-element.986), channel_id=1, source_target_pairs={{32,0},{64,32},{96,64},{128,96},{160,128},{192,160},{224,192},{256... | collective-permute-start | bytes 3080 | tf_op jit(solution)/shard_map/ppermute | solution.py:22
  279.1 3.0 collective-permute-done.33
  283.2 4.3 collective-permute-start.34
  288.8 3.4 collective-permute-done.35
  293.7 4.6 scatter.239
  299.1 107.2 %all-reduce = (f32[]{:T(128)}, f32[]{:T(128)}) all-reduce(f32[]{:T(128)} %get-tuple-element.811, f32[]{:T(128)} %get-tuple-element.810), channel_id=1, replica_groups=mesh['gx'=16,'gy'=4,'gz'=8] {'gx','gy','gz'}, use_global_device_ids=true, to_apply=%region_2.15 | all-reduce | flops 2 | bytes 16 | tf_op jit(solution)/shard_map/psum | solution.py:165
  408.4 94.4 %psum.58 = f32[]{:T(128)} all-reduce(f32[]{:T(128)} %get-tuple-element.862), channel_id=1, replica_groups=mesh['gx'=16,'gy'=4,'gz'=8] {'gx','gy','gz'}, use_global_device_ids=true, to_apply=%region_6.19 | all-reduce | flops 1 | bytes 8 | tf_op jit(solution)/shard_map/psum | solution.py:165
  507.7 4.2 collective-permute-start.36
  513.9 3.2 collective-permute-done.37
  517.5 3.9 collective-permute-start.38
  522.8 3.0 collective-permute-done.39
  530.3 3.7 collective-permute-done.41
  535.5 4.6 scatter.249
  540.9 104.3 %psum.59 = f32[]{:T(128)} all-reduce(f32[]{:T(128)} %fusion.31), channel_id=1, replica_groups=mesh['gx'=16,'gy'=4,'gz'=8] {'gx','gy','gz'}, use_global_device_ids=true, to_apply=%region_8.21 | all-reduce | flops 1 | bytes 8 | tf_op jit(solution)/shard_map/psum | solution.py:182
  647.9 94.4 %psum.60 = f32[]{:T(128)} all-reduce(f32[]{:T(128)} %get-tuple-element.859), channel_id=1, replica_groups=mesh['gx'=16,'gy'=4,'gz'=8] {'gx','gy','gz'}, use_global_device_ids=true, to_apply=%region_10.23 | all-reduce | flops 1 | bytes 8 | tf_op jit(solution)/shard_map/psum | solution.py:165
  747.1 4.2 collective-permute-start.42
  753.3 3.2 collective-permute-done.43
  757.0 2.7 collective-permute-start.44
  761.1 3.0 collective-permute-done.45
  765.2 2.2 collective-permute-start.46
  768.7 3.9 collective-permute-done.47
  774.1 4.6 scatter.259
  779.5 103.8 %psum.61 = f32[]{:T(128)} all-reduce(f32[]{:T(128)} %fusion.33), channel_id=1, replica_groups=mesh['gx'=16,'gy'=4,'gz'=8] {'gx','gy','gz'}, use_global_device_ids=true, to_apply=%region_12.25 | all-reduce | flops 1 | bytes 8 | tf_op jit(solution)/shard_map/psum | solution.py:182
  886.0 94.7 %psum.62 = f32[]{:T(128)} all-reduce(f32[]{:T(128)} %get-tuple-element.856), channel_id=1, replica_groups=mesh['gx'=16,'gy'=4,'gz'=8] {'gx','gy','gz'}, use_global_device_ids=true, to_apply=%region_14.27 | all-reduce | flops 1 | bytes 8 | tf_op jit(solution)/shard_map/psum | solution.py:165
  985.5 4.2 collective-permute-start.48
  991.7 3.2 collective-permute-done.49
  995.3 2.8 collective-permute-start.50
  999.5 3.0 collective-permute-done.51
  1003.6 2.2 collective-permute-start.52
  1007.1 3.9 collective-permute-done.53
  1012.5 4.6 scatter.269
  1018.9 103.9 %psum.63 = f32[]{:T(128)} all-reduce(f32[]{:T(128)} %fusion.35), channel_id=1, replica_groups=mesh['gx'=16,'gy'=4,'gz'=8] {'gx','gy','gz'}, use_global_device_ids=true, to_apply=%region_16.29 | all-reduce | flops 1 | bytes 8 | tf_op jit(solution)/shard_map/psum | solution.py:182
  (531 shorter events, 132.6 us)
Async XLA Ops:
  1.9 10.9 copy-start.5
  2.1 27.2 %collective-permute-start = (f32[1,768]{1,0:T(1,128)S(1)}, f32[1,768]{1,0:T(1,128)S(1)}, u32[]{:S(2)}, u32[]{:S(2)}) collective-permute-start(f32[1,768]{1,0:T(1,128)S(1)} %get-tuple-element.945), channel_id=1, source_target_pairs={{0,32},{32,64},{64,96},{96,128},{128,160},{160,192},{192,224},{224... | collective-permute-start | bytes 9224 | tf_op jit(solution)/shard_map/ppermute | solution.py:19
  6.6 22.7 %collective-permute-start.1 = (f32[1,768]{1,0:T(1,128)S(1)}, f32[1,768]{1,0:T(1,128)S(1)}, u32[]{:S(2)}, u32[]{:S(2)}) collective-permute-start(f32[1,768]{1,0:T(1,128)S(1)} %get-tuple-element.946), channel_id=1, source_target_pairs={{32,0},{64,32},{96,64},{128,96},{160,128},{192,160},{224,192},{256... | collective-permute-start | bytes 9224 | tf_op jit(solution)/shard_map/ppermute | solution.py:22
  12.8 0.7 copy-start.6
  12.9 0.7 copy-start.7
  13.9 12.1 %collective-permute-start.24 = (f32[1,256]{1,0:T(1,128)S(1)}, f32[1,256]{1,0:T(1,128)S(1)}, u32[]{:S(2)}, u32[]{:S(2)}) collective-permute-start(f32[1,256]{1,0:T(1,128)S(1)} %get-tuple-element.997), channel_id=1, source_target_pairs={{0,32},{32,64},{64,96},{96,128},{128,160},{160,192},{192,224},{224... | collective-permute-start | bytes 3080 | tf_op jit(solution)/shard_map/ppermute | solution.py:19
  15.8 10.5 collective-permute-start.25
  26.7 8.7 collective-permute-start.26
  28.1 7.3 collective-permute-start.27
  30.0 5.5 collective-permute-start.2
  34.1 4.4 collective-permute-start.3
  44.0 2.6 collective-permute-start.4
  45.3 4.3 collective-permute-start.5
  71.4 0.9 copy-start
  76.0 0.7 copy-start.4
  79.4 15.9 %collective-permute-start.6 = (f32[1,768]{1,0:T(1,128)S(1)}, f32[1,768]{1,0:T(1,128)S(1)}, u32[]{:S(2)}, u32[]{:S(2)}) collective-permute-start(f32[1,768]{1,0:T(1,128)S(1)} %get-tuple-element.937), channel_id=1, source_target_pairs={{0,32},{32,64},{64,96},{96,128},{128,160},{160,192},{192,224},{224... | collective-permute-start | bytes 9224 | tf_op jit(solution)/shard_map/ppermute | solution.py:19
  81.6 13.7 %collective-permute-start.7 = (f32[1,768]{1,0:T(1,128)S(1)}, f32[1,768]{1,0:T(1,128)S(1)}, u32[]{:S(2)}, u32[]{:S(2)}) collective-permute-start(f32[1,768]{1,0:T(1,128)S(1)} %get-tuple-element.938), channel_id=1, source_target_pairs={{32,0},{64,32},{96,64},{128,96},{160,128},{192,160},{224,192},{256... | collective-permute-start | bytes 9224 | tf_op jit(solution)/shard_map/ppermute | solution.py:22
  95.9 4.9 collective-permute-start.8
  99.2 4.4 collective-permute-start.9
  109.1 5.4 collective-permute-start.10
  113.1 6.2 collective-permute-start.11
  150.5 20.8 %collective-permute-start.12 = (f32[1,768]{1,0:T(1,128)S(1)}, f32[1,768]{1,0:T(1,128)S(1)}, u32[]{:S(2)}, u32[]{:S(2)}) collective-permute-start(f32[1,768]{1,0:T(1,128)S(1)} %get-tuple-element.929), channel_id=1, source_target_pairs={{0,32},{32,64},{64,96},{96,128},{128,160},{160,192},{192,224},{224... | collective-permute-start | bytes 9224 | tf_op jit(solution)/shard_map/ppermute | solution.py:19
  152.4 18.9 %collective-permute-start.13 = (f32[1,768]{1,0:T(1,128)S(1)}, f32[1,768]{1,0:T(1,128)S(1)}, u32[]{:S(2)}, u32[]{:S(2)}) collective-permute-start(f32[1,768]{1,0:T(1,128)S(1)} %get-tuple-element.930), channel_id=1, source_target_pairs={{32,0},{64,32},{96,64},{128,96},{160,128},{192,160},{224,192},{256... | collective-permute-start | bytes 9224 | tf_op jit(solution)/shard_map/ppermute | solution.py:22
  165.2 11.8 %collective-permute-start.28 = (f32[1,128]{1,0:T(1,128)S(1)}, f32[1,128]{1,0:T(1,128)S(1)}, u32[]{:S(2)}, u32[]{:S(2)}) collective-permute-start(f32[1,128]{1,0:T(1,128)S(1)} %get-tuple-element.995), channel_id=1, source_target_pairs={{0,1},{1,2},{2,3},{3,4},{4,5},{5,6},{6,7},{8,9},{9,10},{10,11},{11... | collective-permute-start | bytes 1544 | tf_op jit(solution)/shard_map/ppermute | solution.py:19
  170.0 7.0 collective-permute-start.29
  171.9 5.1 collective-permute-start.14
  175.2 4.4 collective-permute-start.15
  185.1 5.6 collective-permute-start.16
  189.4 4.3 collective-permute-start.17
  216.0 0.7 copy-start.3
  217.2 14.7 %collective-permute-start.18 = (f32[1,256]{1,0:T(1,128)S(1)}, f32[1,256]{1,0:T(1,128)S(1)}, u32[]{:S(2)}, u32[]{:S(2)}) collective-permute-start(f32[1,256]{1,0:T(1,128)S(1)} %get-tuple-element.991), channel_id=1, source_target_pairs={{0,32},{32,64},{64,96},{96,128},{128,160},{160,192},{192,224},{224... | collective-permute-start | bytes 3080 | tf_op jit(solution)/shard_map/ppermute | solution.py:19
  219.2 13.6 %collective-permute-start.19 = (f32[1,256]{1,0:T(1,128)S(1)}, f32[1,256]{1,0:T(1,128)S(1)}, u32[]{:S(2)}, u32[]{:S(2)}) collective-permute-start(f32[1,256]{1,0:T(1,128)S(1)} %get-tuple-element.992), channel_id=1, source_target_pairs={{32,0},{64,32},{96,64},{128,96},{160,128},{192,160},{224,192},{256... | collective-permute-start | bytes 3080 | tf_op jit(solution)/shard_map/ppermute | solution.py:22
  233.2 3.1 collective-permute-start.20
  234.9 4.3 collective-permute-start.21
  240.3 11.0 collective-permute-start.22
  243.9 7.4 collective-permute-start.23
  261.1 13.8 %collective-permute-start.30 = (f32[1,256]{1,0:T(1,128)S(1)}, f32[1,256]{1,0:T(1,128)S(1)}, u32[]{:S(2)}, u32[]{:S(2)}) collective-permute-start(f32[1,256]{1,0:T(1,128)S(1)} %get-tuple-element.985), channel_id=1, source_target_pairs={{0,32},{32,64},{64,96},{96,128},{128,160},{160,192},{192,224},{224... | collective-permute-start | bytes 3080 | tf_op jit(solution)/shard_map/ppermute | solution.py:19
  263.0 12.7 %collective-permute-start.31 = (f32[1,256]{1,0:T(1,128)S(1)}, f32[1,256]{1,0:T(1,128)S(1)}, u32[]{:S(2)}, u32[]{:S(2)}) collective-permute-start(f32[1,256]{1,0:T(1,128)S(1)} %get-tuple-element.986), channel_id=1, source_target_pairs={{32,0},{64,32},{96,64},{128,96},{160,128},{192,160},{224,192},{256... | collective-permute-start | bytes 3080 | tf_op jit(solution)/shard_map/ppermute | solution.py:22
  276.1 3.0 collective-permute-start.32
  277.8 4.3 collective-permute-start.33
  283.2 5.6 collective-permute-start.34
  287.5 4.7 collective-permute-start.35
  507.7 6.2 collective-permute-start.36
  511.9 5.2 collective-permute-start.37
  517.5 5.3 collective-permute-start.38
  521.5 4.3 collective-permute-start.39
  527.1 3.2 collective-permute-start.40
  529.0 5.0 collective-permute-start.41
  747.1 6.2 collective-permute-start.42
  751.4 5.2 collective-permute-start.43
  757.0 4.1 collective-permute-start.44
  759.8 4.3 collective-permute-start.45
  765.2 3.5 collective-permute-start.46
  767.4 5.2 collective-permute-start.47
  778.8 105.9 %copy-start.2 = (f32[1,2,1,4,8,8,8]{6,5,4,3,1,2,0:T(8,128)S(1)}, f32[1,2,1,4,8,8,8]{6,5,4,3,1,2,0:T(8,128)}, u32[]{:S(2)}) copy-start(f32[1,2,1,4,8,8,8]{6,5,4,3,1,2,0:T(8,128)} %get-tuple-element.861) | copy-start | bytes 49156
  985.5 6.2 collective-permute-start.48
  989.7 5.2 collective-permute-start.49
  995.3 4.2 collective-permute-start.50
  998.2 4.3 collective-permute-start.51
  1003.6 3.5 collective-permute-start.52
  1005.8 5.2 collective-permute-start.53
  1124.1 1.0 copy-start.1
where the time goes:
time: 1140 us; the launch traced here: 1130 us
  blocking collectives  703 us (62%)
  starting transfers between devices  176 us (15%)
  local copies, waits for them, and re-layouts  148 us (13%)
  waiting for transfers between devices  60.7 us (5%)
  matrix products  17.8 us (2%)
  between operations  13.6 us (1%)
    psum x4, blocking collectives, norm_weighted_mass(): return lax.psum(local_inner(residual_vec, precond_vec), ('gx', 'gy', 'gz'))  391 us
    psum x3, blocking collectives, body(): lax.psum(local_inner(search, applied), ('gx', 'gy', 'gz'))  312 us
    scatter x54, local copies, waits for them, and re-layouts, place_face(): return values.at[selector].set(update)  98.6 us
    ppermute x27, starting transfers between devices, extended(): lax.ppermute(lax.slice_in_dim(block, 0, width, axis=dim), axis, backward)  95.5 us
    ppermute x27, starting transfers between devices, extended(): lax.ppermute(lax.slice_in_dim(block, block.shape[dim] - width, None, axis...  80.1 us
    ppermute x27, waiting for transfers between devices, extended(): lax.ppermute(lax.slice_in_dim(block, 0, width, axis=dim), axis, backward)  60.7 us
  transfers between devices with their start and end apart: 54, of which 21 were waited for; matrix products, arithmetic and copies ran while one was open for 1% of the time, Pallas kernels for 0%

commit v1 on v0

--- a/solution.py
+++ b/solution.py
@@ -162,7 +162,7 @@
         return jnp.sum(first * second / multiplicity)
 
     def norm_weighted_mass(residual_vec, precond_vec):
-        return lax.psum(local_inner(residual_vec, precond_vec), ("gx", "gy", "gz"))
+        return lax.psum(lax.psum(local_inner(residual_vec, precond_vec), "gx"), ("gy", "gz"))
 
     pressure = jnp.zeros_like(source)
     residual = source

time: 1140 us -> 1330 us (1.17)
  blocking collectives: 703 us -> 864 us
  starting transfers between devices: 176 us -> 215 us
    psum x3 -> x4, blocking collectives: 312 us -> 428 us  [body(): lax.psum(local_inner(search, applied), ('gx', 'gy', 'gz'))]
    psum x4 -> x8, blocking collectives: 391 us -> 436 us  [the longest x4 252 us: norm_weighted_mass(): lax.psum(lax.psum(local_inner(residual_vec, precond_vec), 'gx'), ('gy', '...]
    ppermute x27, starting transfers between devices: 95.5 us -> 115 us  [extended(): lax.ppermute(lax.slice_in_dim(block, 0, width, axis=dim), axis, backward)]
    ppermute x27, starting transfers between devices: 80.1 us -> 99.9 us  [extended(): lax.ppermute(lax.slice_in_dim(block, block.shape[dim] - width, None, axis...]
where the time goes in v1:
time: 1330 us; the launch traced here: 1320 us
  blocking collectives  864 us (65%)
  starting transfers between devices  215 us (16%)
  local copies, waits for them, and re-layouts  148 us (11%)
  waiting for transfers between devices  50.8 us (4%)
  matrix products  17.9 us (1%)
  between operations  13.6 us (1%)
    psum x4, blocking collectives, body(): lax.psum(local_inner(search, applied), ('gx', 'gy', 'gz'))  428 us
    psum x4, blocking collectives, norm_weighted_mass(): lax.psum(lax.psum(local_inner(residual_vec, precond_vec), 'gx'), ('gy', '...  252 us
    psum x4, blocking collectives, norm_weighted_mass(): lax.psum(local_inner(residual_vec, precond_vec), 'gx')  184 us
    ppermute x27, starting transfers between devices, extended(): lax.ppermute(lax.slice_in_dim(block, 0, width, axis=dim), axis, backward)  115 us
    ppermute x27, starting transfers between devices, extended(): lax.ppermute(lax.slice_in_dim(block, block.shape[dim] - width, None, axis...  99.9 us
    scatter x54, local copies, waits for them, and re-layouts, place_face(): return values.at[selector].set(update)  98.7 us
    ppermute x27, waiting for transfers between devices, extended(): lax.ppermute(lax.slice_in_dim(block, 0, width, axis=dim), axis, backward)  50.7 us
  transfers between devices with their start and end apart: 54, of which 21 were waited for; matrix products, arithmetic and copies ran while one was open for 1% of the time, Pallas kernels for 0%

profile of v1, /device:TPU:1, one launch (start us, length us, event | category | flops | bytes accessed | tf_op | source)
XLA Modules:
  0.0 1318.2 jit_solution(3516431587018881805)
XLA Ops:
  2.1 4.5 collective-permute-start
  6.6 6.2 collective-permute-start.1
  15.8 9.7 collective-permute-start.25
  30.0 4.0 collective-permute-start.2
  35.4 3.0 collective-permute-done.3
  46.6 3.0 collective-permute-done.5
  51.0 2.6 scatter.186
  54.8 15.4 %scatter.189 = f32[3,2,1,4,8,8,8]{6,5,4,3,1,0,2:T(8,128)S(1)} dynamic-update-slice(f32[3,2,1,4,8,8,8]{6,5,4,3,1,0,2:T(8,128)S(1)} %scatter.186, f32[3,2,1,4,8,8,1]{6,5,4,3,1,0,2:T(8,128)S(1)} %copy.186, s32[]{:T(128)} %constant.1319.clone.1, s32[]{:T(128)} %constant.1319.clone.1, s32[]{:T(128)} %constant.1319.clone.1, s32[]{:T(128)} %constant.1319.clone.1, s32[]{:T(128)} %constant.1319.clone.1, ...) | dynamic-update-slice | bytes 12292 | tf_op jit(solution)/shard_map/scatter | solution.py:63
  76.8 2.4 fusion.2
  79.4 2.2 collective-permute-start.6
  81.7 12.9 collective-permute-start.7
  95.9 3.2 collective-permute-start.8
  100.9 2.8 collective-permute-done.9
  109.2 4.0 collective-permute-start.10
  114.6 4.7 collective-permute-done.11
  120.1 2.1 copy.201
  122.2 2.6 scatter.196
  127.6 15.4 %scatter.199 = f32[3,2,1,4,8,8,8]{6,5,4,3,1,0,2:T(8,128)S(1)} dynamic-update-slice(f32[3,2,1,4,8,8,8]{6,5,4,3,1,0,2:T(8,128)S(1)} %scatter.196, f32[3,2,1,4,8,8,1]{6,5,4,3,1,0,2:T(8,128)S(1)} %copy.203, s32[]{:T(128)} %constant.1319.clone.1, s32[]{:T(128)} %constant.1319.clone.1, s32[]{:T(128)} %constant.1319.clone.1, s32[]{:T(128)} %constant.1319.clone.1, s32[]{:T(128)} %constant.1319.clone.1, ...) | dynamic-update-slice | bytes 12292 | tf_op jit(solution)/shard_map/scatter | solution.py:63
  148.1 2.2 fusion.5
  152.5 12.7 collective-permute-start.13
  165.2 4.8 collective-permute-start.28
  172.0 3.2 collective-permute-start.14
  177.0 2.6 collective-permute-done.15
  185.2 4.3 collective-permute-start.16
  190.8 3.0 collective-permute-done.17
  195.1 2.6 scatter.206
  199.0 15.4 %scatter.209 = f32[3,2,1,4,8,8,8]{6,5,4,3,1,0,2:T(8,128)S(1)} dynamic-update-slice(f32[3,2,1,4,8,8,8]{6,5,4,3,1,0,2:T(8,128)S(1)} %scatter.206, f32[3,2,1,4,8,8,1]{6,5,4,3,1,0,2:T(8,128)S(1)} %copy.220, s32[]{:T(128)} %constant.1319.clone.1, s32[]{:T(128)} %constant.1319.clone.1, s32[]{:T(128)} %constant.1319.clone.1, s32[]{:T(128)} %constant.1319.clone.1, s32[]{:T(128)} %constant.1319.clone.1, ...) | dynamic-update-slice | bytes 12292 | tf_op jit(solution)/shard_map/scatter | solution.py:63
  219.2 12.8 collective-permute-start.19
  236.2 3.0 collective-permute-done.21
  240.3 3.6 collective-permute-start.22
  246.7 4.6 scatter.229
  252.8 4.8 scatter.219
  263.0 11.8 collective-permute-start.31
  279.2 3.0 collective-permute-done.33
  283.2 4.3 collective-permute-start.34
  288.8 3.4 collective-permute-done.35
  293.7 4.6 scatter.239
  299.1 53.5 %psum.84 = f32[]{:T(128)} all-reduce(f32[]{:T(128)} %get-tuple-element.811), channel_id=1, replica_groups=mesh['gx'=16,'gy'=4,'gz'=8] {'gx'}, use_global_device_ids=true, to_apply=%region_2.15 | all-reduce | flops 1 | bytes 8 | tf_op jit(solution)/shard_map/psum | solution.py:165
  352.7 62.8 %psum.85 = f32[]{:T(128)} all-reduce(f32[]{:T(128)} %psum.84), channel_id=1, replica_groups=mesh['gx'=16,'gy'=4,'gz'=8] {'gy','gz'}, use_global_device_ids=true, to_apply=%region_3.16 | all-reduce | flops 1 | bytes 8 | tf_op jit(solution)/shard_map/psum | solution.py:165
  415.5 111.4 %psum.86 = f32[]{:T(128)} all-reduce(f32[]{:T(128)} %get-tuple-element.810), channel_id=1, replica_groups=mesh['gx'=16,'gy'=4,'gz'=8] {'gx','gy','gz'}, use_global_device_ids=true, to_apply=%region_5.18 | all-reduce | flops 1 | bytes 8 | tf_op jit(solution)/shard_map/psum | solution.py:182
  529.0 43.4 %psum.87 = f32[]{:T(128)} all-reduce(f32[]{:T(128)} %get-tuple-element.860), channel_id=1, replica_groups=mesh['gx'=16,'gy'=4,'gz'=8] {'gx'}, use_global_device_ids=true, to_apply=%region_7.20 | all-reduce | flops 1 | bytes 8 | tf_op jit(solution)/shard_map/psum | solution.py:165
  572.4 63.5 %psum.88 = f32[]{:T(128)} all-reduce(f32[]{:T(128)} %psum.87), channel_id=1, replica_groups=mesh['gx'=16,'gy'=4,'gz'=8] {'gy','gz'}, use_global_device_ids=true, to_apply=%region_8.21 | all-reduce | flops 1 | bytes 8 | tf_op jit(solution)/shard_map/psum | solution.py:165
  640.7 13.9 %collective-permute-start.36 = (f32[1,256]{1,0:T(1,128)S(1)}, f32[1,256]{1,0:T(1,128)S(1)}, u32[]{:S(2)}, u32[]{:S(2)}) collective-permute-start(f32[1,256]{1,0:T(1,128)S(1)} %get-tuple-element.977), channel_id=1, source_target_pairs={{0,32},{32,64},{64,96},{96,128},{128,160},{160,192},{192,224},{224... | collective-permute-start | bytes 3080 | tf_op jit(solution)/shard_map/ppermute | solution.py:19
  654.6 8.6 collective-permute-start.37
  667.1 3.0 collective-permute-done.39
  674.7 3.0 collective-permute-done.41
  679.1 4.6 scatter.249
  684.5 105.7 %psum.89 = f32[]{:T(128)} all-reduce(f32[]{:T(128)} %fusion.31), channel_id=1, replica_groups=mesh['gx'=16,'gy'=4,'gz'=8] {'gx','gy','gz'}, use_global_device_ids=true, to_apply=%region_10.23 | all-reduce | flops 1 | bytes 8 | tf_op jit(solution)/shard_map/psum | solution.py:182
  793.0 43.4 %psum.90 = f32[]{:T(128)} all-reduce(f32[]{:T(128)} %get-tuple-element.857), channel_id=1, replica_groups=mesh['gx'=16,'gy'=4,'gz'=8] {'gx'}, use_global_device_ids=true, to_apply=%region_12.25 | all-reduce | flops 1 | bytes 8 | tf_op jit(solution)/shard_map/psum | solution.py:165
  836.4 62.6 %psum.91 = f32[]{:T(128)} all-reduce(f32[]{:T(128)} %psum.90), channel_id=1, replica_groups=mesh['gx'=16,'gy'=4,'gz'=8] {'gy','gz'}, use_global_device_ids=true, to_apply=%region_13.26 | all-reduce | flops 1 | bytes 8 | tf_op jit(solution)/shard_map/psum | solution.py:165
  903.8 12.4 collective-permute-start.42
  916.2 8.6 collective-permute-start.43
  928.7 3.0 collective-permute-done.45
  936.0 3.0 collective-permute-done.47
  940.4 4.6 scatter.259
  945.8 105.5 %psum.92 = f32[]{:T(128)} all-reduce(f32[]{:T(128)} %fusion.33), channel_id=1, replica_groups=mesh['gx'=16,'gy'=4,'gz'=8] {'gx','gy','gz'}, use_global_device_ids=true, to_apply=%region_15.28 | all-reduce | flops 1 | bytes 8 | tf_op jit(solution)/shard_map/psum | solution.py:182
  1054.1 43.4 %psum.93 = f32[]{:T(128)} all-reduce(f32[]{:T(128)} %get-tuple-element.854), channel_id=1, replica_groups=mesh['gx'=16,'gy'=4,'gz'=8] {'gx'}, use_global_device_ids=true, to_apply=%region_17.30 | all-reduce | flops 1 | bytes 8 | tf_op jit(solution)/shard_map/psum | solution.py:165
  1097.5 63.1 %psum.94 = f32[]{:T(128)} all-reduce(f32[]{:T(128)} %psum.93), channel_id=1, replica_groups=mesh['gx'=16,'gy'=4,'gz'=8] {'gy','gz'}, use_global_device_ids=true, to_apply=%region_18.31 | all-reduce | flops 1 | bytes 8 | tf_op jit(solution)/shard_map/psum | solution.py:165
  1165.3 12.4 collective-permute-start.48
  1177.7 8.6 collective-permute-start.49
  1190.2 3.0 collective-permute-done.51
  1197.5 3.0 collective-permute-done.53
  1201.9 4.6 scatter.269
  1208.3 105.5 %psum.95 = f32[]{:T(128)} all-reduce(f32[]{:T(128)} %fusion.35), channel_id=1, replica_groups=mesh['gx'=16,'gy'=4,'gz'=8] {'gx','gy','gz'}, use_global_device_ids=true, to_apply=%region_20.33 | all-reduce | flops 1 | bytes 8 | tf_op jit(solution)/shard_map/psum | solution.py:182
  (536 shorter events, 136.8 us)
Async XLA Ops:
  1.9 10.9 copy-start.5
  2.1 27.2 %collective-permute-start = (f32[1,768]{1,0:T(1,128)S(1)}, f32[1,768]{1,0:T(1,128)S(1)}, u32[]{:S(2)}, u32[]{:S(2)}) collective-permute-start(f32[1,768]{1,0:T(1,128)S(1)} %get-tuple-element.943), channel_id=1, source_target_pairs={{0,32},{32,64},{64,96},{96,128},{128,160},{160,192},{192,224},{224... | collective-permute-start | bytes 9224 | tf_op jit(solution)/shard_map/ppermute | solution.py:19
  6.6 22.7 %collective-permute-start.1 = (f32[1,768]{1,0:T(1,128)S(1)}, f32[1,768]{1,0:T(1,128)S(1)}, u32[]{:S(2)}, u32[]{:S(2)}) collective-permute-start(f32[1,768]{1,0:T(1,128)S(1)} %get-tuple-element.944), channel_id=1, source_target_pairs={{32,0},{64,32},{96,64},{128,96},{160,128},{192,160},{224,192},{256... | collective-permute-start | bytes 9224 | tf_op jit(solution)/shard_map/ppermute | solution.py:22
  12.8 0.7 copy-start.6
  12.9 0.7 copy-start.7
  13.9 12.1 collective-permute-start.24
  15.8 10.5 collective-permute-start.25
  26.7 8.7 collective-permute-start.26
  28.1 7.3 collective-permute-start.27
  30.0 5.5 collective-permute-start.2
  34.1 4.4 collective-permute-start.3
  44.0 2.6 collective-permute-start.4
  45.3 4.3 collective-permute-start.5
  71.4 0.9 copy-start
  76.1 0.7 copy-start.4
  79.4 15.9 %collective-permute-start.6 = (f32[1,768]{1,0:T(1,128)S(1)}, f32[1,768]{1,0:T(1,128)S(1)}, u32[]{:S(2)}, u32[]{:S(2)}) collective-permute-start(f32[1,768]{1,0:T(1,128)S(1)} %get-tuple-element.935), channel_id=1, source_target_pairs={{0,32},{32,64},{64,96},{96,128},{128,160},{160,192},{192,224},{224... | collective-permute-start | bytes 9224 | tf_op jit(solution)/shard_map/ppermute | solution.py:19
  81.7 13.7 %collective-permute-start.7 = (f32[1,768]{1,0:T(1,128)S(1)}, f32[1,768]{1,0:T(1,128)S(1)}, u32[]{:S(2)}, u32[]{:S(2)}) collective-permute-start(f32[1,768]{1,0:T(1,128)S(1)} %get-tuple-element.936), channel_id=1, source_target_pairs={{32,0},{64,32},{96,64},{128,96},{160,128},{192,160},{224,192},{256... | collective-permute-start | bytes 9224 | tf_op jit(solution)/shard_map/ppermute | solution.py:22
  95.9 4.9 collective-permute-start.8
  99.3 4.4 collective-permute-start.9
  109.2 5.4 collective-permute-start.10
  113.2 6.2 collective-permute-start.11
  150.5 20.8 %collective-permute-start.12 = (f32[1,768]{1,0:T(1,128)S(1)}, f32[1,768]{1,0:T(1,128)S(1)}, u32[]{:S(2)}, u32[]{:S(2)}) collective-permute-start(f32[1,768]{1,0:T(1,128)S(1)} %get-tuple-element.927), channel_id=1, source_target_pairs={{0,32},{32,64},{64,96},{96,128},{128,160},{160,192},{192,224},{224... | collective-permute-start | bytes 9224 | tf_op jit(solution)/shard_map/ppermute | solution.py:19
  152.5 18.9 %collective-permute-start.13 = (f32[1,768]{1,0:T(1,128)S(1)}, f32[1,768]{1,0:T(1,128)S(1)}, u32[]{:S(2)}, u32[]{:S(2)}) collective-permute-start(f32[1,768]{1,0:T(1,128)S(1)} %get-tuple-element.928), channel_id=1, source_target_pairs={{32,0},{64,32},{96,64},{128,96},{160,128},{192,160},{224,192},{256... | collective-permute-start | bytes 9224 | tf_op jit(solution)/shard_map/ppermute | solution.py:22
  165.2 11.8 collective-permute-start.28
  170.1 6.9 collective-permute-start.29
  172.0 5.1 collective-permute-start.14
  175.3 4.4 collective-permute-start.15
  185.2 5.6 collective-permute-start.16
  189.4 4.3 collective-permute-start.17
  216.0 0.7 copy-start.3
  217.2 14.7 %collective-permute-start.18 = (f32[1,256]{1,0:T(1,128)S(1)}, f32[1,256]{1,0:T(1,128)S(1)}, u32[]{:S(2)}, u32[]{:S(2)}) collective-permute-start(f32[1,256]{1,0:T(1,128)S(1)} %get-tuple-element.989), channel_id=1, source_target_pairs={{0,32},{32,64},{64,96},{96,128},{128,160},{160,192},{192,224},{224... | collective-permute-start | bytes 3080 | tf_op jit(solution)/shard_map/ppermute | solution.py:19
  219.2 13.6 %collective-permute-start.19 = (f32[1,256]{1,0:T(1,128)S(1)}, f32[1,256]{1,0:T(1,128)S(1)}, u32[]{:S(2)}, u32[]{:S(2)}) collective-permute-start(f32[1,256]{1,0:T(1,128)S(1)} %get-tuple-element.990), channel_id=1, source_target_pairs={{32,0},{64,32},{96,64},{128,96},{160,128},{192,160},{224,192},{256... | collective-permute-start | bytes 3080 | tf_op jit(solution)/shard_map/ppermute | solution.py:22
  233.2 3.0 collective-permute-start.20
  234.9 4.3 collective-permute-start.21
  240.3 11.0 collective-permute-start.22
  243.9 7.4 collective-permute-start.23
  261.1 13.8 %collective-permute-start.30 = (f32[1,256]{1,0:T(1,128)S(1)}, f32[1,256]{1,0:T(1,128)S(1)}, u32[]{:S(2)}, u32[]{:S(2)}) collective-permute-start(f32[1,256]{1,0:T(1,128)S(1)} %get-tuple-element.983), channel_id=1, source_target_pairs={{0,32},{32,64},{64,96},{96,128},{128,160},{160,192},{192,224},{224... | collective-permute-start | bytes 3080 | tf_op jit(solution)/shard_map/ppermute | solution.py:19
  263.0 12.7 collective-permute-start.31
  276.1 3.0 collective-permute-start.32
  277.8 4.3 collective-permute-start.33
  283.2 5.6 collective-permute-start.34
  287.5 4.7 collective-permute-start.35
  640.7 22.4 %collective-permute-start.36 = (f32[1,256]{1,0:T(1,128)S(1)}, f32[1,256]{1,0:T(1,128)S(1)}, u32[]{:S(2)}, u32[]{:S(2)}) collective-permute-start(f32[1,256]{1,0:T(1,128)S(1)} %get-tuple-element.977), channel_id=1, source_target_pairs={{0,32},{32,64},{64,96},{96,128},{128,160},{160,192},{192,224},{224... | collective-permute-start | bytes 3080 | tf_op jit(solution)/shard_map/ppermute | solution.py:19
  654.6 9.4 collective-permute-start.37
  664.4 2.7 collective-permute-start.38
  665.7 4.3 collective-permute-start.39
  671.4 3.3 collective-permute-start.40
  673.4 4.3 collective-permute-start.41
  903.8 21.0 %collective-permute-start.42 = (f32[1,256]{1,0:T(1,128)S(1)}, f32[1,256]{1,0:T(1,128)S(1)}, u32[]{:S(2)}, u32[]{:S(2)}) collective-permute-start(f32[1,256]{1,0:T(1,128)S(1)} %get-tuple-element.971), channel_id=1, source_target_pairs={{0,32},{32,64},{64,96},{96,128},{128,160},{160,192},{192,224},{224... | collective-permute-start | bytes 3080 | tf_op jit(solution)/shard_map/ppermute | solution.py:19
  916.2 9.4 collective-permute-start.43
  926.0 2.7 collective-permute-start.44
  927.4 4.3 collective-permute-start.45
  932.8 3.1 collective-permute-start.46
  934.6 4.3 collective-permute-start.47
  945.1 107.6 %copy-start.2 = (f32[1,2,1,4,8,8,8]{6,5,4,3,1,2,0:T(8,128)S(1)}, f32[1,2,1,4,8,8,8]{6,5,4,3,1,2,0:T(8,128)}, u32[]{:S(2)}) copy-start(f32[1,2,1,4,8,8,8]{6,5,4,3,1,2,0:T(8,128)} %get-tuple-element.859) | copy-start | bytes 49156
  1165.3 21.0 %collective-permute-start.48 = (f32[1,256]{1,0:T(1,128)S(1)}, f32[1,256]{1,0:T(1,128)S(1)}, u32[]{:S(2)}, u32[]{:S(2)}) collective-permute-start(f32[1,256]{1,0:T(1,128)S(1)} %get-tuple-element.965), channel_id=1, source_target_pairs={{0,32},{32,64},{64,96},{96,128},{128,160},{160,192},{192,224},{224... | collective-permute-start | bytes 3080 | tf_op jit(solution)/shard_map/ppermute | solution.py:19
  1177.7 9.4 collective-permute-start.49
  1187.5 2.7 collective-permute-start.50
  1188.9 4.3 collective-permute-start.51
  1194.3 3.1 collective-permute-start.52
  1196.2 4.3 collective-permute-start.53
  1315.2 1.0 copy-start.1
